TPU v7x, 32 devices: a whole 2x2x4 slice. The times are simulated.
32 devices in a mesh: blk: 4 (over x, core), grp: 8 (over z, y).
Axes of the slice: x: 2, y: 2, z: 4, core: 2. Of those that a mesh axis runs over, the one named last changes fastest.
Arguments:
- picture_vectors: bfloat16 [12288, 1152], P(('blk', 'grp')), may hold values from -2.3570226 to 2.3570226
- text_vectors: bfloat16 [12288, 1152], P(('blk', 'grp')), may hold values from -2.3570226 to 2.3570226
- matching_text_position: int32 [32, 384], P(('blk', 'grp')), may hold values from 0 to 383, each once within a row
- natural_scale_exponent: float32 [1], replicated, may hold values from 1.5 to 2.3
- offset_added_before_sigmoid: float32 [1], replicated, may hold values from -3 to -1
Outputs:
- image_grad: bfloat16 [12288, 1152], P(('blk', 'grp'))
- caption_grad: bfloat16 [12288, 1152], P(('blk', 'grp'))
Inputs may be any that keep to these rules, and one draw needn't show every extreme that they name: `matching_text_position`: each row of positives names every position 0 .. 383 exactly once.
All inputs are finite; a program needn't handle non-finite values.
Results may differ from a plain program's by a relative error of at most 0.0059.
Values may be sent and summed in bfloat16 or wider, within the bound.
A program may use at most 64 MiB of HBM per device.

v0:
```python
import jax
import jax.numpy as jnp
from jax import lax
from jax.sharding import PartitionSpec as P

STEPS = 4


def padded(shard, sides, width):
    for axis, dim in sides:
        devices, length = (lax.axis_size(axis), shard.shape[dim])
        up = [(i, (i + 1) % devices) for i in range(devices)]
        down = [(j, i) for i, j in up]
        last = lax.slice_in_dim(shard, length - width, length, axis=dim)
        initial = lax.slice_in_dim(shard, 0, width, axis=dim)
        before = lax.ppermute(last, axis, up)
        after = lax.ppermute(initial, axis, down)
        shard = jnp.concatenate([before, shard, after], axis=dim)
    return shard


def unit_rows(raw_rows):
    values = raw_rows.astype(jnp.float32)
    inverse_norm = lax.rsqrt(jnp.sum(values * values, axis=1, keepdims=True) + 1e-06)
    return (values * inverse_norm, inverse_norm)


def cross_dot_products(
    picture_entry_slab, window_width_along_diagonal, exponentiated_scale, rotation_offset
):
    cosine_table = lax.dot_general(
        picture_entry_slab,
        window_width_along_diagonal,
        (((1,), (1,)), ((), ())),
        preferred_element_type=jnp.float32,
    )
    return exponentiated_scale * cosine_table + rotation_offset


def sigmoid_cost_coefficients(agreement_table, label_polarity, exponentiated_scale):
    derivative_wrt_presigmoid = -label_polarity * jax.nn.sigmoid(-label_polarity * agreement_table)
    return (exponentiated_scale * derivative_wrt_presigmoid).astype(jnp.bfloat16)


def finish(unit_flat, inverse_norm, direction):
    cosine_table = jnp.sum(unit_flat * direction, axis=1, keepdims=True)
    return (inverse_norm * (direction - unit_flat * cosine_table)).astype(jnp.bfloat16)


def local(
    picture_vectors,
    text_vectors,
    matching_text_position,
    natural_scale_exponent,
    offset_added_before_sigmoid,
):
    total_row_count = picture_vectors.shape[0]
    midpoint_entries = total_row_count // 2
    exponentiated_scale = jnp.exp(natural_scale_exponent[0])
    rotation_offset = offset_added_before_sigmoid[0]
    image_flat, image_inverse = unit_rows(picture_vectors)
    caption_flat, caption_inverse = unit_rows(text_vectors)
    unit_length_picture_vectors = image_flat.astype(jnp.bfloat16)
    normalized_caption_rows = caption_flat.astype(jnp.bfloat16)
    columns = lax.broadcasted_iota(jnp.int32, (total_row_count, total_row_count), 1)
    first_labels = jnp.where(
        (columns + midpoint_entries) % total_row_count == matching_text_position[0][:, None],
        1.0,
        -1.0,
    ).astype(jnp.float32)
    circulating_text_storage = jnp.concatenate(
        [normalized_caption_rows[midpoint_entries:], normalized_caption_rows[:midpoint_entries]],
        axis=0,
    )
    image_gradient_total = jnp.zeros(picture_vectors.shape, jnp.float32)
    pieces = []
    for rotation in range(STEPS):
        if rotation > 0:
            padded_embeddings = padded(
                circulating_text_storage, ((("blk", "grp"), 0),), midpoint_entries
            )
            circulating_text_storage = jnp.concatenate(
                [
                    padded_embeddings[total_row_count + midpoint_entries :],
                    padded_embeddings[:midpoint_entries],
                ],
                axis=0,
            )
        label_polarity = first_labels if rotation == 0 else -1.0
        coupling_coefficient = sigmoid_cost_coefficients(
            cross_dot_products(
                unit_length_picture_vectors,
                circulating_text_storage,
                exponentiated_scale,
                rotation_offset,
            ),
            label_polarity,
            exponentiated_scale,
        )
        image_gradient_total = image_gradient_total + jnp.dot(
            coupling_coefficient, circulating_text_storage, preferred_element_type=jnp.float32
        )
        text_piece = lax.dot_general(
            coupling_coefficient,
            unit_length_picture_vectors,
            (((0,), (0,)), ((), ())),
            preferred_element_type=jnp.float32,
        )
        pieces.append(text_piece)
    running = pieces[STEPS - 1]
    for rotation in range(STEPS - 2, -1, -1):
        flipped = jnp.concatenate([running[midpoint_entries:], running[:midpoint_entries]], axis=0)
        moved_back = padded(flipped, ((("blk", "grp"), 0),), midpoint_entries)
        running = (
            jnp.concatenate(
                [moved_back[:midpoint_entries], moved_back[total_row_count + midpoint_entries :]],
                axis=0,
            )
            + pieces[rotation]
        )
    second_half = running[:midpoint_entries]
    first_half = running[midpoint_entries:]
    caption_sum = jnp.concatenate([first_half, second_half], axis=0)
    image_grad = finish(image_flat, image_inverse, image_gradient_total)
    caption_grad = finish(caption_flat, caption_inverse, caption_sum)
    return (image_grad, caption_grad)


def solution(mesh):
    in_specs = (P(("blk", "grp"), None), P(("blk", "grp"), None), P(("blk", "grp"), None), P(), P())
    out_specs = (P(("blk", "grp"), None), P(("blk", "grp"), None))
    return jax.shard_map(local, mesh=mesh, in_specs=in_specs, out_specs=out_specs, check_vma=False)
```

profile of v0, /device:TPU:0, one launch (start us, length us, event | category | flops | bytes accessed | tf_op | source)
XLA Modules:
  0.0 197.2 jit_solution(268888505268621665)
XLA Ops:
  0.6 1.4 fusion.15
  2.1 1.5 fusion.2
  3.6 6.5 %collective-permute-start = (bf16[192,1152]{1,0:T(8,128)(2,1)S(1)}, bf16[192,1152]{1,0:T(8,128)(2,1)S(1)}, u32[]{:S(2)}, u32[]{:S(2)}) collective-permute-start(bf16[192,1152]{1,0:T(8,128)(2,1)S(1)} %get-tuple-element.10), channel_id=1, source_target_pairs={{1,0},{2,1},{3,2},{4,3},{5,4},{6,5},{7,6},{8,7},{9,8},{10,9},{11,1... | collective-permute-start | bytes 1327112 | tf_op jit(solution)/shard_map/ppermute | solution.py:17
  10.3 16.7 %collective-permute-done = bf16[192,1152]{1,0:T(8,128)(2,1)S(1)} collective-permute-done((bf16[192,1152]{1,0:T(8,128)(2,1)S(1)}, bf16[192,1152]{1,0:T(8,128)(2,1)S(1)}, u32[]{:S(2)}, u32[]{:S(2)}) %collective-permute-start) | collective-permute-done | bytes 442400 | tf_op jit(solution)/shard_map/ppermute | solution.py:17
  27.0 1.6 collective-permute-start.2
  30.5 0.8 fusion.42
  31.3 7.8 %collective-permute-done.2 = bf16[192,1152]{1,0:T(8,128)(2,1)S(1)} collective-permute-done((bf16[192,1152]{1,0:T(8,128)(2,1)S(1)}, bf16[192,1152]{1,0:T(8,128)(2,1)S(1)}, u32[]{:S(2)}, u32[]{:S(2)}) %collective-permute-start.2) | collective-permute-done | bytes 442400 | tf_op jit(solution)/shard_map/ppermute | solution.py:17
  39.1 9.2 %collective-permute-start.4 = (bf16[192,1152]{1,0:T(8,128)(2,1)S(1)}, bf16[192,1152]{1,0:T(8,128)(2,1)S(1)}, u32[]{:S(2)}, u32[]{:S(2)}) collective-permute-start(bf16[192,1152]{1,0:T(8,128)(2,1)S(1)} %collective-permute-done.2), channel_id=1, source_target_pairs={{1,0},{2,1},{3,2},{4,3},{5,4},{6,5},{7,6},{8,7},{9,8},{10,9},{11,1... | collective-permute-start | bytes 1327112 | tf_op jit(solution)/shard_map/ppermute | solution.py:17
  49.1 9.0 %collective-permute-done.4 = bf16[192,1152]{1,0:T(8,128)(2,1)S(1)} collective-permute-done((bf16[192,1152]{1,0:T(8,128)(2,1)S(1)}, bf16[192,1152]{1,0:T(8,128)(2,1)S(1)}, u32[]{:S(2)}, u32[]{:S(2)}) %collective-permute-start.4) | collective-permute-done | bytes 442400 | tf_op jit(solution)/shard_map/ppermute | solution.py:17
  58.1 7.4 %collective-permute-done.5 = bf16[192,1152]{1,0:T(8,128)(2,1)S(1)} collective-permute-done((bf16[192,1152]{1,0:T(8,128)(2,1)S(1)}, bf16[192,1152]{1,0:T(8,128)(2,1)S(1)}, u32[]{:S(2)}, u32[]{:S(2)}) %collective-permute-start.5) | collective-permute-done | bytes 442400 | tf_op jit(solution)/shard_map/ppermute | solution.py:16
  65.5 0.8 fusion.43
  66.3 0.8 fusion.56
  67.2 8.6 %collective-permute-start.7 = (f32[192,1152]{1,0:T(8,128)S(1)}, f32[192,1152]{1,0:T(8,128)S(1)}, u32[]{:S(2)}, u32[]{:S(2)}) collective-permute-start(f32[192,1152]{1,0:T(8,128)S(1)} %get-tuple-element.9), channel_id=1, source_target_pairs={{1,0},{2,1},{3,2},{4,3},{5,4},{6,5},{7,6},{8,7},{9,8},{10,9},{11,1... | collective-permute-start | bytes 2654216 | tf_op jit(solution)/shard_map/ppermute | solution.py:17
  76.0 0.8 fusion.44
  76.7 31.9 %collective-permute-done.7 = f32[192,1152]{1,0:T(8,128)S(1)} collective-permute-done((f32[192,1152]{1,0:T(8,128)S(1)}, f32[192,1152]{1,0:T(8,128)S(1)}, u32[]{:S(2)}, u32[]{:S(2)}) %collective-permute-start.7) | collective-permute-done | bytes 884768 | tf_op jit(solution)/shard_map/ppermute | solution.py:17
  109.7 6.8 %collective-permute-start.9 = (f32[192,1152]{1,0:T(8,128)S(1)}, f32[192,1152]{1,0:T(8,128)S(1)}, u32[]{:S(2)}, u32[]{:S(2)}) collective-permute-start(f32[192,1152]{1,0:T(8,128)S(1)} %get-tuple-element.7), channel_id=1, source_target_pairs={{1,0},{2,1},{3,2},{4,3},{5,4},{6,5},{7,6},{8,7},{9,8},{10,9},{11,1... | collective-permute-start | bytes 2654216 | tf_op jit(solution)/shard_map/ppermute | solution.py:17
  116.5 0.8 fusion.45
  118.6 32.5 %collective-permute-done.9 = f32[192,1152]{1,0:T(8,128)S(1)} collective-permute-done((f32[192,1152]{1,0:T(8,128)S(1)}, f32[192,1152]{1,0:T(8,128)S(1)}, u32[]{:S(2)}, u32[]{:S(2)}) %collective-permute-start.9) | collective-permute-done | bytes 884768 | tf_op jit(solution)/shard_map/ppermute | solution.py:17
  152.1 5.1 %collective-permute-start.11 = (f32[192,1152]{1,0:T(8,128)S(1)}, f32[192,1152]{1,0:T(8,128)S(1)}, u32[]{:S(2)}, u32[]{:S(2)}) collective-permute-start(f32[192,1152]{1,0:T(8,128)S(1)} %get-tuple-element.5), channel_id=1, source_target_pairs={{1,0},{2,1},{3,2},{4,3},{5,4},{6,5},{7,6},{8,7},{9,8},{10,9},{11,1... | collective-permute-start | bytes 2654216 | tf_op jit(solution)/shard_map/ppermute | solution.py:17
  157.2 0.8 fusion.6
  158.0 1.3 fusion.9
  159.3 34.2 %collective-permute-done.11 = f32[192,1152]{1,0:T(8,128)S(1)} collective-permute-done((f32[192,1152]{1,0:T(8,128)S(1)}, f32[192,1152]{1,0:T(8,128)S(1)}, u32[]{:S(2)}, u32[]{:S(2)}) %collective-permute-start.11) | collective-permute-done | bytes 884768 | tf_op jit(solution)/shard_map/ppermute | solution.py:17
  194.5 1.0 copy-done.1
  195.9 1.3 fusion.14
  (40 shorter events, 6.6 us)
Async XLA Ops:
  2.1 8.0 %copy-start = (bf16[384,1152]{1,0:T(8,128)(2,1)S(1)}, bf16[384,1152]{1,0:T(8,128)(2,1)}, u32[]{:S(2)}) copy-start(bf16[384,1152]{1,0:T(8,128)(2,1)} %param.5) | copy-start | bytes 2654212
  3.5 26.5 %copy-start.2 = (s32[1,384]{1,0:T(1,128)S(1)}, s32[1,384]{1,0:T(1,128)}, u32[]{:S(2)}) copy-start(s32[1,384]{1,0:T(1,128)} %param.7) | copy-start | bytes 4612
  3.6 23.4 %collective-permute-start = (bf16[192,1152]{1,0:T(8,128)(2,1)S(1)}, bf16[192,1152]{1,0:T(8,128)(2,1)S(1)}, u32[]{:S(2)}, u32[]{:S(2)}) collective-permute-start(bf16[192,1152]{1,0:T(8,128)(2,1)S(1)} %get-tuple-element.10), channel_id=1, source_target_pairs={{1,0},{2,1},{3,2},{4,3},{5,4},{6,5},{7,6},{8,7},{9,8},{10,9},{11,1... | collective-permute-start | bytes 1327112 | tf_op jit(solution)/shard_map/ppermute | solution.py:17
  10.1 20.0 %collective-permute-start.1 = (bf16[192,1152]{1,0:T(8,128)(2,1)S(1)}, bf16[192,1152]{1,0:T(8,128)(2,1)S(1)}, u32[]{:S(2)}, u32[]{:S(2)}) collective-permute-start(bf16[192,1152]{1,0:T(8,128)(2,1)S(1)} %get-tuple-element.11), channel_id=1, source_target_pairs={{0,1},{1,2},{2,3},{3,4},{4,5},{5,6},{6,7},{7,8},{8,9},{9,10},{10,1... | collective-permute-start | bytes 1327112 | tf_op jit(solution)/shard_map/ppermute | solution.py:16
  27.0 12.1 %collective-permute-start.2 = (bf16[192,1152]{1,0:T(8,128)(2,1)S(1)}, bf16[192,1152]{1,0:T(8,128)(2,1)S(1)}, u32[]{:S(2)}, u32[]{:S(2)}) collective-permute-start(bf16[192,1152]{1,0:T(8,128)(2,1)S(1)} %collective-permute-done), channel_id=1, source_target_pairs={{1,0},{2,1},{3,2},{4,3},{5,4},{6,5},{7,6},{8,7},{9,8},{10,9},{11,1... | collective-permute-start | bytes 1327112 | tf_op jit(solution)/shard_map/ppermute | solution.py:17
  30.0 18.9 %collective-permute-start.3 = (bf16[192,1152]{1,0:T(8,128)(2,1)S(1)}, bf16[192,1152]{1,0:T(8,128)(2,1)S(1)}, u32[]{:S(2)}, u32[]{:S(2)}) collective-permute-start(bf16[192,1152]{1,0:T(8,128)(2,1)S(1)} %collective-permute-done.1), channel_id=1, source_target_pairs={{0,1},{1,2},{2,3},{3,4},{4,5},{5,6},{6,7},{7,8},{8,9},{9,10},{10,1... | collective-permute-start | bytes 1327112 | tf_op jit(solution)/shard_map/ppermute | solution.py:16
  39.1 19.0 %collective-permute-start.4 = (bf16[192,1152]{1,0:T(8,128)(2,1)S(1)}, bf16[192,1152]{1,0:T(8,128)(2,1)S(1)}, u32[]{:S(2)}, u32[]{:S(2)}) collective-permute-start(bf16[192,1152]{1,0:T(8,128)(2,1)S(1)} %collective-permute-done.2), channel_id=1, source_target_pairs={{1,0},{2,1},{3,2},{4,3},{5,4},{6,5},{7,6},{8,7},{9,8},{10,9},{11,1... | collective-permute-start | bytes 1327112 | tf_op jit(solution)/shard_map/ppermute | solution.py:17
  49.0 16.5 %collective-permute-start.5 = (bf16[192,1152]{1,0:T(8,128)(2,1)S(1)}, bf16[192,1152]{1,0:T(8,128)(2,1)S(1)}, u32[]{:S(2)}, u32[]{:S(2)}) collective-permute-start(bf16[192,1152]{1,0:T(8,128)(2,1)S(1)} %collective-permute-done.3), channel_id=1, source_target_pairs={{0,1},{1,2},{2,3},{3,4},{4,5},{5,6},{6,7},{7,8},{8,9},{9,10},{10,1... | collective-permute-start | bytes 1327112 | tf_op jit(solution)/shard_map/ppermute | solution.py:16
  67.2 41.4 %collective-permute-start.7 = (f32[192,1152]{1,0:T(8,128)S(1)}, f32[192,1152]{1,0:T(8,128)S(1)}, u32[]{:S(2)}, u32[]{:S(2)}) collective-permute-start(f32[192,1152]{1,0:T(8,128)S(1)} %get-tuple-element.9), channel_id=1, source_target_pairs={{1,0},{2,1},{3,2},{4,3},{5,4},{6,5},{7,6},{8,7},{9,8},{10,9},{11,1... | collective-permute-start | bytes 2654216 | tf_op jit(solution)/shard_map/ppermute | solution.py:17
  75.8 33.0 %collective-permute-start.6 = (f32[192,1152]{1,0:T(8,128)S(1)}, f32[192,1152]{1,0:T(8,128)S(1)}, u32[]{:S(2)}, u32[]{:S(2)}) collective-permute-start(f32[192,1152]{1,0:T(8,128)S(1)} %get-tuple-element.8), channel_id=1, source_target_pairs={{0,1},{1,2},{2,3},{3,4},{4,5},{5,6},{6,7},{7,8},{8,9},{9,10},{10,1... | collective-permute-start | bytes 2654216 | tf_op jit(solution)/shard_map/ppermute | solution.py:16
  109.7 41.4 %collective-permute-start.9 = (f32[192,1152]{1,0:T(8,128)S(1)}, f32[192,1152]{1,0:T(8,128)S(1)}, u32[]{:S(2)}, u32[]{:S(2)}) collective-permute-start(f32[192,1152]{1,0:T(8,128)S(1)} %get-tuple-element.7), channel_id=1, source_target_pairs={{1,0},{2,1},{3,2},{4,3},{5,4},{6,5},{7,6},{8,7},{9,8},{10,9},{11,1... | collective-permute-start | bytes 2654216 | tf_op jit(solution)/shard_map/ppermute | solution.py:17
  116.5 34.7 %collective-permute-start.8 = (f32[192,1152]{1,0:T(8,128)S(1)}, f32[192,1152]{1,0:T(8,128)S(1)}, u32[]{:S(2)}, u32[]{:S(2)}) collective-permute-start(f32[192,1152]{1,0:T(8,128)S(1)} %get-tuple-element.6), channel_id=1, source_target_pairs={{0,1},{1,2},{2,3},{3,4},{4,5},{5,6},{6,7},{7,8},{8,9},{9,10},{10,1... | collective-permute-start | bytes 2654216 | tf_op jit(solution)/shard_map/ppermute | solution.py:16
  152.1 41.4 %collective-permute-start.11 = (f32[192,1152]{1,0:T(8,128)S(1)}, f32[192,1152]{1,0:T(8,128)S(1)}, u32[]{:S(2)}, u32[]{:S(2)}) collective-permute-start(f32[192,1152]{1,0:T(8,128)S(1)} %get-tuple-element.5), channel_id=1, source_target_pairs={{1,0},{2,1},{3,2},{4,3},{5,4},{6,5},{7,6},{8,7},{9,8},{10,9},{11,1... | collective-permute-start | bytes 2654216 | tf_op jit(solution)/shard_map/ppermute | solution.py:17
  157.2 36.4 %collective-permute-start.10 = (f32[192,1152]{1,0:T(8,128)S(1)}, f32[192,1152]{1,0:T(8,128)S(1)}, u32[]{:S(2)}, u32[]{:S(2)}) collective-permute-start(f32[192,1152]{1,0:T(8,128)S(1)} %get-tuple-element.4), channel_id=1, source_target_pairs={{0,1},{1,2},{2,3},{3,4},{4,5},{5,6},{6,7},{7,8},{8,9},{9,10},{10,1... | collective-permute-start | bytes 2654216 | tf_op jit(solution)/shard_map/ppermute | solution.py:16
  194.4 1.2 copy-start.1
where the time goes:
time: 197 us
  waiting for transfers between devices  140 us (71%)
  starting transfers between devices  38.3 us (19%)
  matrix products  8.87 us (5%)
  other arithmetic  6.18 us (3%)
  between operations  2.2 us (1%)
    ppermute x6, waiting for transfers between devices, padded(): after = lax.ppermute(initial, axis, down)  132 us
    ppermute x6, starting transfers between devices, padded(): after = lax.ppermute(initial, axis, down)  37.8 us
    ppermute x6, waiting for transfers between devices, padded(): before = lax.ppermute(last, axis, up)  7.74 us
  transfers between devices with their start and end apart: 12, of which 10 were waited for; matrix products, arithmetic and copies ran while one was open for 4% of the time, Pallas kernels for 0%

commit v1 on v0

v1 whole, which is shorter than its diff:
```python
import functools

import jax
import jax.numpy as jnp
from jax import lax
from jax.experimental import pallas as pl
from jax.experimental.pallas import tpu as pltpu
from jax.sharding import PartitionSpec as P

CHUNKS = 2
NORM_ROWS = 48
MESH = pl.DeviceIdType.MESH

A0, A1, A2, A3, B0, B1, B2, B3 = range(8)
(
    OWN_A_PAIR,
    OWN_A_FAR,
    A1_FAR,
    A2_PAIR,
    OWN_B_FAR,
    B2_PAIR,
    SUM_B1,
    SUM_B3,
    SUM_A3,
    SUM_A1,
    SUM_A2,
    SUM_B2,
) = range(12)


def kernel(
    groups,
    total,
    image_ref,
    text_ref,
    position_ref,
    exponent_ref,
    offset_ref,
    image_out,
    text_out,
    image_unit,
    captions,
    coefs,
    partial,
    staged,
    returned,
    direction,
    image_inverse,
    text_inverse,
    send_sem,
    recv_sem,
):
    rows, width = image_ref.shape
    half = rows // 2
    chunk = half // CHUNKS
    me = lax.axis_index("blk") * groups + lax.axis_index("grp")
    parity = lax.rem(me, 2)
    step = 1 - 2 * parity

    def place(index):
        index = lax.rem(index + total, total)
        return (index // groups, lax.rem(index, groups))

    pair = place(me + step)
    ahead = place(me + 2 * step)
    behind = place(me - 2 * step)

    barrier = pltpu.get_barrier_semaphore()
    for device in (pair, ahead, behind):
        pl.semaphore_signal(barrier, inc=1, device_id=device, device_id_type=MESH)

    start_a = pl.multiple_of(parity * half, half)
    start_b = pl.multiple_of(half - parity * half, half)

    def piece(c):
        return pl.ds(c * chunk, chunk)

    def message(name, c, source, target, device):
        return pltpu.make_async_remote_copy(
            src_ref=source.at[piece(c)],
            dst_ref=target.at[piece(c)],
            send_sem=send_sem.at[name, c],
            recv_sem=recv_sem.at[name, c],
            device_id=device,
            device_id_type=MESH,
        )

    routes = {
        OWN_A_PAIR: (captions.at[A0], captions.at[B1], pair),
        OWN_A_FAR: (captions.at[A0], captions.at[A2], ahead),
        A1_FAR: (captions.at[A1], captions.at[A3], ahead),
        A2_PAIR: (captions.at[A2], captions.at[B3], pair),
        OWN_B_FAR: (captions.at[B0], captions.at[B2], behind),
        B2_PAIR: (captions.at[B2], captions.at[A1], pair),
        SUM_B1: (staged.at[0], returned.at[0], pair),
        SUM_B3: (staged.at[1], returned.at[1], pair),
        SUM_A3: (staged.at[2], returned.at[2], behind),
        SUM_A1: (staged.at[3], returned.at[3], pair),
        SUM_A2: (staged.at[4], returned.at[4], behind),
        SUM_B2: (staged.at[5], returned.at[5], ahead),
    }

    def send(name, c):
        message(name, c, *routes[name]).start()

    def receive(name, c):
        message(name, c, *routes[name]).wait_recv()

    def normalize(source, inverse, slot_ref, source_start):
        def body(i, carry):
            at = pl.multiple_of(i * NORM_ROWS, NORM_ROWS)
            here = pl.ds(pl.multiple_of(source_start + at, NORM_ROWS), NORM_ROWS)
            values = source[here, :].astype(jnp.float32)
            scale = lax.rsqrt(jnp.sum(values * values, axis=1, keepdims=True) + 1e-06)
            inverse[here, :] = scale
            slot_ref[pl.ds(at, NORM_ROWS), :] = (values * scale).astype(jnp.bfloat16)
            return carry

        lax.fori_loop(0, slot_ref.shape[0] // NORM_ROWS, body, 0)

    normalize(text_ref, text_inverse, captions.at[B0], start_b)
    normalize(text_ref, text_inverse, captions.at[A0], start_a)
    pl.semaphore_wait(barrier, 3)
    for c in range(CHUNKS):
        send(OWN_B_FAR, c)
        send(OWN_A_FAR, c)
    send(OWN_A_PAIR, 0)
    normalize(image_ref, image_inverse, image_unit, 0)

    scale = jnp.exp(jnp.full((1, rows), exponent_ref[0], jnp.float32))
    offset = offset_ref[0]

    def tile(slot, c, first_row=None):
        text = captions[slot, piece(c), :]
        logit = (
            lax.dot_general(
                text,
                image_unit[...],
                (((1,), (1,)), ((), ())),
                preferred_element_type=jnp.float32,
            )
            * scale
            + offset
        )
        if first_row is None:
            coef = scale * jax.nn.sigmoid(logit)
        else:
            row = lax.broadcasted_iota(jnp.int32, logit.shape, 0) + first_row + c * chunk
            polarity = jnp.where(row == position_ref[0:1, :], 1.0, -1.0)
            coef = scale * (-polarity * jax.nn.sigmoid(-polarity * logit))
        coef = coef.astype(jnp.bfloat16)
        coefs[slot, piece(c), :] = coef
        return jnp.dot(coef, image_unit[...], preferred_element_type=jnp.float32)

    for c in range(CHUNKS):
        receive(OWN_B_FAR, c)
        send(B2_PAIR, c)
        if c + 1 < CHUNKS:
            send(OWN_A_PAIR, c + 1)
        receive(OWN_A_FAR, c)
        send(A2_PAIR, c)
    for c in range(CHUNKS):
        receive(OWN_A_PAIR, c)
        staged[0, piece(c), :] = tile(B1, c).astype(jnp.bfloat16)
        send(SUM_B1, c)
        receive(B2_PAIR, c)
        send(A1_FAR, c)
    for c in range(CHUNKS):
        partial[0, piece(c), :] = tile(A1, c)
        partial[1, piece(c), :] = tile(A2, c)
        partial[2, piece(c), :] = tile(B2, c)
        receive(A2_PAIR, c)
        staged[1, piece(c), :] = tile(B3, c).astype(jnp.bfloat16)
        send(SUM_B3, c)
    for c in range(CHUNKS):
        receive(A1_FAR, c)
        staged[2, piece(c), :] = tile(A3, c).astype(jnp.bfloat16)
        send(SUM_A3, c)
    for c in range(CHUNKS):
        partial[3, piece(c), :] = tile(A0, c, start_a)
        partial[4, piece(c), :] = tile(B0, c, start_b)
    def relay(name, c, source, buffer, slot, part):
        receive(source, c)
        arrived = returned[buffer, piece(c), :].astype(jnp.float32)
        staged[slot, piece(c), :] = (arrived + partial[part, piece(c), :]).astype(
            jnp.bfloat16
        )
        send(name, c)

    for c in range(CHUNKS):
        relay(SUM_A1, c, SUM_A3, 2, 3, 0)
        relay(SUM_A2, c, SUM_B3, 1, 4, 1)
    for c in range(CHUNKS):
        relay(SUM_B2, c, SUM_A1, 3, 5, 2)

    tile_width = 384 if width % 384 == 0 else 128

    def accumulate(i, carry):
        lanes = pl.ds(pl.multiple_of(i * tile_width, 128), tile_width)
        result = jnp.zeros((rows, tile_width), jnp.float32)
        for slot in range(8):
            result += lax.dot_general(
                coefs[slot],
                captions[slot, :, lanes],
                (((0,), (0,)), ((), ())),
                preferred_element_type=jnp.float32,
            )
        direction[:, lanes] = result
        return carry

    lax.fori_loop(0, width // tile_width, accumulate, 0)

    def finish(source, inverse, here, value):
        scale = inverse[here, :]
        flat = source[here, :].astype(jnp.float32) * scale
        cosine = jnp.sum(flat * value, axis=1, keepdims=True)
        return (scale * (value - flat * cosine)).astype(jnp.bfloat16)

    def finish_images(i, carry):
        here = pl.ds(pl.multiple_of(i * NORM_ROWS, NORM_ROWS), NORM_ROWS)
        image_out[here, :] = finish(image_ref, image_inverse, here, direction[here, :])
        return carry

    lax.fori_loop(0, rows // NORM_ROWS, finish_images, 0)

    def finish_text(c, start, part, buffers):
        def body(i, carry):
            at = pl.multiple_of(c * chunk + i * NORM_ROWS, NORM_ROWS)
            local = pl.ds(at, NORM_ROWS)
            here = pl.ds(pl.multiple_of(start + at, NORM_ROWS), NORM_ROWS)
            value = partial[part, local, :]
            for buffer in buffers:
                value += returned[buffer, local, :].astype(jnp.float32)
            text_out[here, :] = finish(text_ref, text_inverse, here, value)
            return carry

        lax.fori_loop(0, chunk // NORM_ROWS, body, 0)

    for c in range(CHUNKS):
        receive(SUM_B1, c)
        receive(SUM_A2, c)
        finish_text(c, start_a, 3, (0, 4))
    for c in range(CHUNKS):
        receive(SUM_B2, c)
        finish_text(c, start_b, 4, (5,))
    for name in routes:
        for c in range(CHUNKS):
            message(name, c, *routes[name]).wait_send()


def solution(mesh):
    groups = mesh.shape["grp"]
    total = mesh.shape["blk"] * groups

    def local(images, texts, positions, exponent, offset):
        rows, width = images.shape
        half = rows // 2
        vmem = pl.BlockSpec(memory_space=pltpu.VMEM)
        smem = pl.BlockSpec(memory_space=pltpu.SMEM)
        return pl.pallas_call(
            functools.partial(kernel, groups, total),
            out_shape=(
                jax.ShapeDtypeStruct((rows, width), jnp.bfloat16),
                jax.ShapeDtypeStruct((rows, width), jnp.bfloat16),
            ),
            in_specs=[vmem, vmem, vmem, smem, smem],
            out_specs=(vmem, vmem),
            scratch_shapes=[
                pltpu.VMEM((rows, width), jnp.bfloat16),
                pltpu.VMEM((8, half, width), jnp.bfloat16),
                pltpu.VMEM((8, half, rows), jnp.bfloat16),
                pltpu.VMEM((5, half, width), jnp.float32),
                pltpu.VMEM((6, half, width), jnp.bfloat16),
                pltpu.VMEM((6, half, width), jnp.bfloat16),
                pltpu.VMEM((rows, width), jnp.float32),
                pltpu.VMEM((rows, 1), jnp.float32),
                pltpu.VMEM((rows, 1), jnp.float32),
                pltpu.SemaphoreType.DMA((12, CHUNKS)),
                pltpu.SemaphoreType.DMA((12, CHUNKS)),
            ],
            compiler_params=pltpu.CompilerParams(
                collective_id=0, has_side_effects=True, vmem_limit_bytes=48 * 1024 * 1024
            ),
        )(images, texts, positions, exponent, offset)

    shard = P(("blk", "grp"), None)
    return jax.shard_map(
        local,
        mesh=mesh,
        in_specs=(shard, shard, shard, P(), P()),
        out_specs=(shard, shard),
        check_vma=False,
    )
```

time: 197 us -> 80.8 us (0.41)
  waiting for transfers between devices: 140 us -> 0 us
  Pallas kernels: 0 us -> 74.5 us
  starting transfers between devices: 38.3 us -> 0 us
  matrix products: 8.87 us -> 0 us
  other arithmetic: 6.18 us -> 0 us
  local copies, waits for them, and re-layouts: 1.82 us -> 4.16 us
    ppermute x12 -> x0, waiting for transfers between devices: 140 us -> none  [the longest x6 132 us: padded(): after = lax.ppermute(initial, axis, down)]
    pallas_call x0 -> x1, Pallas kernels: none -> 74.5 us  [local(): pl.pallas_call(functools.partial(kernel, groups, total), out_shape=(jax.S...]
    ppermute x12 -> x0, starting transfers between devices: 38.3 us -> none  [the longest x6 37.8 us: padded(): after = lax.ppermute(initial, axis, down)]
    dot_general x12 -> x0, matrix products: 8.87 us -> none  [the longest x4 3.12 us: cross_dot_products(): lax.dot_general(picture_entry_slab, window_width_along_diagonal, (((1,),...]
    convert_element_type x3 -> x0, other arithmetic: 4.08 us -> none  [the longest x2 2.62 us: finish(): (inverse_norm * (direction - unit_flat * cosine_table)).astype(jnp.bfloat16)]
    unnamed x9 -> x8, local copies, waits for them, and re-layouts: 1.15 us -> 4.16 us
    reduce_sum x3 -> x0, other arithmetic: 2.05 us -> none  [the longest x2 1.67 us: unit_rows(): jnp.sum(values * values, axis=1, keepdims=True) + 1e-06]
  transfers between devices with their start and end apart: 12 -> 0, of which waited for: 10 -> 0; matrix products, arithmetic and copies ran while one was open for 4% -> 0% of each run, Pallas kernels for 0% -> 0%
where the time goes in v1:
time: 80.8 us; the launch traced here: 80.6 us
  Pallas kernels  74.5 us (92%)
  local copies, waits for them, and re-layouts  4.16 us (5%)
  between operations  1.97 us (2%)
    pallas_call x1, Pallas kernels, local(): pl.pallas_call(functools.partial(kernel, groups, total), out_shape=(jax.S...  74.5 us
    unnamed x8, local copies, waits for them, and re-layouts  4.16 us

profile of v1, /device:TPU:0, one launch (start us, length us, event | category | flops | bytes accessed | tf_op | source)
XLA Modules:
  0.0 80.6 jit_solution(12973668625762247414)
XLA Ops:
  0.6 0.0 copy-start.2
  1.9 0.0 copy-done.2
  2.0 0.0 copy-start
  2.0 1.2 %copy-done = bf16[384,1152]{1,0:T(8,128)(2,1)S(1)} copy-done((bf16[384,1152]{1,0:T(8,128)(2,1)S(1)}, bf16[384,1152]{1,0:T(8,128)(2,1)}, u32[]{:S(2)}) %copy-start) | copy-done | bytes 884760
  3.1 0.0 copy-start.1
  3.1 1.2 %copy-done.1 = bf16[384,1152]{1,0:T(8,128)(2,1)S(1)} copy-done((bf16[384,1152]{1,0:T(8,128)(2,1)S(1)}, bf16[384,1152]{1,0:T(8,128)(2,1)}, u32[]{:S(2)}) %copy-start.1) | copy-done | bytes 884760
  4.3 74.5 %shard_map.68 = (bf16[384,1152]{1,0:T(8,128)(2,1)S(1)}, bf16[384,1152]{1,0:T(8,128)(2,1)S(1)}) custom-call(bf16[384,1152]{1,0:T(8,128)(2,1)S(1)} %copy-done, bf16[384,1152]{1,0:T(8,128)(2,1)S(1)} %copy-done.1, s32[1,384]{1,0:T(1,128)S(1)} %copy-done.2, f32[1]{0:T(128)S(6)} %copy.9.exponent_ref, f32[1]{0:T(128)S(6)} %copy.10.offset_ref), custom_call_target="tpu_custom_call" | custom-call | tf_op jit(solution)/shard_map/pallas_call | solution.py:260
  78.8 0.9 %copy.11 = bf16[384,1152]{1,0:T(8,128)(2,1)} copy(bf16[384,1152]{1,0:T(8,128)(2,1)S(1)} %get-tuple-element.4) | data formatting | bytes 1769472
  79.7 0.9 %copy.12 = bf16[384,1152]{1,0:T(8,128)(2,1)} copy(bf16[384,1152]{1,0:T(8,128)(2,1)S(1)} %get-tuple-element.5) | data formatting | bytes 1769472
Async XLA Ops:
  0.6 1.3 %copy-start.2 = (s32[1,384]{1,0:T(1,128)S(1)}, s32[1,384]{1,0:T(1,128)}, u32[]{:S(2)}) copy-start(s32[1,384]{1,0:T(1,128)} %position_ref.1) | copy-start | bytes 4612
  2.0 1.2 %copy-start = (bf16[384,1152]{1,0:T(8,128)(2,1)S(1)}, bf16[384,1152]{1,0:T(8,128)(2,1)}, u32[]{:S(2)}) copy-start(bf16[384,1152]{1,0:T(8,128)(2,1)} %image_ref.1) | copy-start | bytes 2654212
  3.1 1.2 %copy-start.1 = (bf16[384,1152]{1,0:T(8,128)(2,1)S(1)}, bf16[384,1152]{1,0:T(8,128)(2,1)}, u32[]{:S(2)}) copy-start(bf16[384,1152]{1,0:T(8,128)(2,1)} %text_ref.1) | copy-start | bytes 2654212

commit v2 on v1

--- a/solution.py
+++ b/solution.py
@@ -7,8 +7,8 @@
 from jax.experimental.pallas import tpu as pltpu
 from jax.sharding import PartitionSpec as P
 
-CHUNKS = 2
-NORM_ROWS = 48
+CHUNKS = 3
+NORM_ROWS = 32
 MESH = pl.DeviceIdType.MESH
 
 A0, A1, A2, A3, B0, B1, B2, B3 = range(8)
@@ -31,13 +31,16 @@
 def kernel(
     groups,
     total,
-    image_ref,
-    text_ref,
-    position_ref,
+    image_hbm,
+    text_hbm,
+    position_hbm,
     exponent_ref,
     offset_ref,
     image_out,
     text_out,
+    image_ref,
+    text_ref,
+    position_ref,
     image_unit,
     captions,
     coefs,
@@ -47,10 +50,11 @@
     direction,
     image_inverse,
     text_inverse,
+    load_sem,
     send_sem,
     recv_sem,
 ):
-    rows, width = image_ref.shape
+    rows, width = image_hbm.shape
     half = rows // 2
     chunk = half // CHUNKS
     me = lax.axis_index("blk") * groups + lax.axis_index("grp")
@@ -71,6 +75,19 @@
 
     start_a = pl.multiple_of(parity * half, half)
     start_b = pl.multiple_of(half - parity * half, half)
+
+    def load(n, source, target):
+        return pltpu.make_async_copy(source, target, load_sem.at[n])
+
+    half_a, half_b = (pl.ds(start_a, half), pl.ds(start_b, half))
+    loads = (
+        load(0, text_hbm.at[half_b], text_ref.at[half_b]),
+        load(1, text_hbm.at[half_a], text_ref.at[half_a]),
+        load(2, image_hbm, image_ref),
+        load(3, position_hbm, position_ref),
+    )
+    for copy in loads:
+        copy.start()
 
     def piece(c):
         return pl.ds(c * chunk, chunk)
@@ -118,13 +135,17 @@
 
         lax.fori_loop(0, slot_ref.shape[0] // NORM_ROWS, body, 0)
 
+    loads[0].wait()
     normalize(text_ref, text_inverse, captions.at[B0], start_b)
+    pl.semaphore_wait(barrier, 3)
+    for c in range(CHUNKS):
+        send(OWN_B_FAR, c)
+    loads[1].wait()
     normalize(text_ref, text_inverse, captions.at[A0], start_a)
-    pl.semaphore_wait(barrier, 3)
-    for c in range(CHUNKS):
-        send(OWN_B_FAR, c)
-        send(OWN_A_FAR, c)
     send(OWN_A_PAIR, 0)
+    send(OWN_A_FAR, 0)
+    for load in loads[2:]:
+        load.wait()
     normalize(image_ref, image_inverse, image_unit, 0)
 
     scale = jnp.exp(jnp.full((1, rows), exponent_ref[0], jnp.float32))
@@ -152,33 +173,6 @@
         coefs[slot, piece(c), :] = coef
         return jnp.dot(coef, image_unit[...], preferred_element_type=jnp.float32)
 
-    for c in range(CHUNKS):
-        receive(OWN_B_FAR, c)
-        send(B2_PAIR, c)
-        if c + 1 < CHUNKS:
-            send(OWN_A_PAIR, c + 1)
-        receive(OWN_A_FAR, c)
-        send(A2_PAIR, c)
-    for c in range(CHUNKS):
-        receive(OWN_A_PAIR, c)
-        staged[0, piece(c), :] = tile(B1, c).astype(jnp.bfloat16)
-        send(SUM_B1, c)
-        receive(B2_PAIR, c)
-        send(A1_FAR, c)
-    for c in range(CHUNKS):
-        partial[0, piece(c), :] = tile(A1, c)
-        partial[1, piece(c), :] = tile(A2, c)
-        partial[2, piece(c), :] = tile(B2, c)
-        receive(A2_PAIR, c)
-        staged[1, piece(c), :] = tile(B3, c).astype(jnp.bfloat16)
-        send(SUM_B3, c)
-    for c in range(CHUNKS):
-        receive(A1_FAR, c)
-        staged[2, piece(c), :] = tile(A3, c).astype(jnp.bfloat16)
-        send(SUM_A3, c)
-    for c in range(CHUNKS):
-        partial[3, piece(c), :] = tile(A0, c, start_a)
-        partial[4, piece(c), :] = tile(B0, c, start_b)
     def relay(name, c, source, buffer, slot, part):
         receive(source, c)
         arrived = returned[buffer, piece(c), :].astype(jnp.float32)
@@ -186,12 +180,6 @@
             jnp.bfloat16
         )
         send(name, c)
-
-    for c in range(CHUNKS):
-        relay(SUM_A1, c, SUM_A3, 2, 3, 0)
-        relay(SUM_A2, c, SUM_B3, 1, 4, 1)
-    for c in range(CHUNKS):
-        relay(SUM_B2, c, SUM_A1, 3, 5, 2)
 
     tile_width = 384 if width % 384 == 0 else 128
 
@@ -208,8 +196,6 @@
         direction[:, lanes] = result
         return carry
 
-    lax.fori_loop(0, width // tile_width, accumulate, 0)
-
     def finish(source, inverse, here, value):
         scale = inverse[here, :]
         flat = source[here, :].astype(jnp.float32) * scale
@@ -221,7 +207,6 @@
         image_out[here, :] = finish(image_ref, image_inverse, here, direction[here, :])
         return carry
 
-    lax.fori_loop(0, rows // NORM_ROWS, finish_images, 0)
 
     def finish_text(c, start, part, buffers):
         def body(i, carry):
@@ -236,6 +221,59 @@
 
         lax.fori_loop(0, chunk // NORM_ROWS, body, 0)
 
+    def forward(arrival, name, c):
+        receive(arrival, c)
+        send(name, c)
+
+    def keep(slot, part, c, first_row=None):
+        partial[part, piece(c), :] = tile(slot, c, first_row)
+
+    def give(arrival, slot, stage, c):
+        receive(arrival, c)
+        staged[stage, piece(c), :] = tile(slot, c).astype(jnp.bfloat16)
+
+    def images():
+        lax.fori_loop(0, width // tile_width, accumulate, 0)
+        lax.fori_loop(0, rows // NORM_ROWS, finish_images, 0)
+
+    for c in range(CHUNKS):
+        forward(OWN_B_FAR, B2_PAIR, c)
+        if c + 1 < CHUNKS:
+            send(OWN_A_FAR, c + 1)
+            send(OWN_A_PAIR, c + 1)
+    for c in range(CHUNKS):
+        forward(B2_PAIR, A1_FAR, c)
+        forward(OWN_A_FAR, A2_PAIR, c)
+    give(OWN_A_PAIR, B1, 0, 0)
+    send(SUM_B1, 0)
+    for c in range(1, CHUNKS):
+        give(OWN_A_PAIR, B1, 0, c)
+
+    for c in range(CHUNKS):
+        keep(A1, 0, c)
+        give(A1_FAR, A3, 2, c)
+        send(SUM_A3, c)
+        give(A2_PAIR, B3, 1, c)
+        send(SUM_B3, c)
+    for c in range(CHUNKS):
+        keep(A2, 1, c)
+        keep(B2, 2, c)
+
+    for c in range(CHUNKS):
+        relay(SUM_A1, c, SUM_A3, 2, 3, 0)
+        relay(SUM_A2, c, SUM_B3, 1, 4, 1)
+    for c in range(1, CHUNKS):
+        send(SUM_B1, c)
+
+    for c in range(CHUNKS):
+        keep(A0, 3, c, start_a)
+        keep(B0, 4, c, start_b)
+
+    for c in range(CHUNKS):
+        relay(SUM_B2, c, SUM_A1, 3, 5, 2)
+
+    images()
+
     for c in range(CHUNKS):
         receive(SUM_B1, c)
         receive(SUM_A2, c)
@@ -243,6 +281,7 @@
     for c in range(CHUNKS):
         receive(SUM_B2, c)
         finish_text(c, start_b, 4, (5,))
+
     for name in routes:
         for c in range(CHUNKS):
             message(name, c, *routes[name]).wait_send()
@@ -256,6 +295,7 @@
         rows, width = images.shape
         half = rows // 2
         vmem = pl.BlockSpec(memory_space=pltpu.VMEM)
+        hbm = pl.BlockSpec(memory_space=pl.ANY)
         smem = pl.BlockSpec(memory_space=pltpu.SMEM)
         return pl.pallas_call(
             functools.partial(kernel, groups, total),
@@ -263,9 +303,12 @@
                 jax.ShapeDtypeStruct((rows, width), jnp.bfloat16),
                 jax.ShapeDtypeStruct((rows, width), jnp.bfloat16),
             ),
-            in_specs=[vmem, vmem, vmem, smem, smem],
+            in_specs=[hbm, hbm, hbm, smem, smem],
             out_specs=(vmem, vmem),
             scratch_shapes=[
+                pltpu.VMEM((rows, width), jnp.bfloat16),
+                pltpu.VMEM((rows, width), jnp.bfloat16),
+                pltpu.VMEM((1, rows), jnp.int32),
                 pltpu.VMEM((rows, width), jnp.bfloat16),
                 pltpu.VMEM((8, half, width), jnp.bfloat16),
                 pltpu.VMEM((8, half, rows), jnp.bfloat16),
@@ -275,11 +318,12 @@
                 pltpu.VMEM((rows, width), jnp.float32),
                 pltpu.VMEM((rows, 1), jnp.float32),
                 pltpu.VMEM((rows, 1), jnp.float32),
+                pltpu.SemaphoreType.DMA((4,)),
                 pltpu.SemaphoreType.DMA((12, CHUNKS)),
                 pltpu.SemaphoreType.DMA((12, CHUNKS)),
             ],
             compiler_params=pltpu.CompilerParams(
-                collective_id=0, has_side_effects=True, vmem_limit_bytes=48 * 1024 * 1024
+                collective_id=0, has_side_effects=True, vmem_limit_bytes=60 * 1024 * 1024
             ),
         )(images, texts, positions, exponent, offset)
 

time: 80.8 us -> 76.1 us (0.942)
  Pallas kernels: 74.5 us -> 70.8 us
  local copies, waits for them, and re-layouts: 4.16 us -> 3.14 us
    pallas_call x1, Pallas kernels: 74.5 us -> 70.8 us  [local(): pl.pallas_call(functools.partial(kernel, groups, total), out_shape=(jax.S...]
    unnamed x8 -> x4, local copies, waits for them, and re-layouts: 4.16 us -> 3.14 us
where the time goes in v2:
time: 76.1 us; the launch traced here: 75.9 us
  Pallas kernels  70.8 us (93%)
  local copies, waits for them, and re-layouts  3.14 us (4%)
  between operations  1.94 us (3%)
    pallas_call x1, Pallas kernels, local(): pl.pallas_call(functools.partial(kernel, groups, total), out_shape=(jax.S...  70.8 us
    unnamed x4, local copies, waits for them, and re-layouts  3.14 us

profile of v2, /device:TPU:0, one launch (start us, length us, event | category | flops | bytes accessed | tf_op | source)
XLA Modules:
  0.0 75.9 jit_solution(14508615713471708579)
XLA Ops:
  1.9 70.8 %shard_map.68 = (bf16[384,1152]{1,0:T(8,128)(2,1)}, bf16[384,1152]{1,0:T(8,128)(2,1)}) custom-call(bf16[384,1152]{1,0:T(8,128)(2,1)} %image_hbm.1, bf16[384,1152]{1,0:T(8,128)(2,1)} %text_hbm.1, s32[1,384]{1,0:T(1,128)} %position_hbm.1, f32[1]{0:T(128)S(6)} %copy.9.exponent_ref, f32[1]{0:T(128)S(6)} %copy.10.offset_ref), custom_call_target="tpu_custom_call" | custom-call | tf_op jit(solution)/shard_map/pallas_call | solution.py:300
  72.7 0.0 copy-start
  72.8 2.2 %copy.11 = bf16[384,1152]{1,0:T(8,128)(2,1)} copy(bf16[384,1152]{1,0:T(8,128)(2,1)} %get-tuple-element.4) | data formatting | bytes 1769472
  75.0 0.0 copy-done
  75.0 0.9 %copy.12 = bf16[384,1152]{1,0:T(8,128)(2,1)} copy(bf16[384,1152]{1,0:T(8,128)(2,1)S(1)} %copy-done) | data formatting | bytes 1769472
Async XLA Ops:
  72.7 2.2 %copy-start = (bf16[384,1152]{1,0:T(8,128)(2,1)S(1)}, bf16[384,1152]{1,0:T(8,128)(2,1)}, u32[]{:S(2)}) copy-start(bf16[384,1152]{1,0:T(8,128)(2,1)} %get-tuple-element.5) | copy-start | bytes 2654212
